TPU v7x, 32 devices: a whole 2x2x4 slice. The times are simulated.
32 devices in a mesh: row: 4 (over z), col: 8 (over y, x, core).
Axes of the slice: x: 2, y: 2, z: 4, core: 2. Of those that a mesh axis runs over, the one named last changes fastest.
Arguments:
- solution: float32 [8, 8, 4, 8, 256], P(None, None, 'row', 'col'), may hold values from -6 to 6
- residual: float32 [8, 8, 4, 8, 256], P(None, None, 'row', 'col'), may hold values from -120 to 120
- direction: float32 [8, 8, 4, 8, 256], P(None, None, 'row', 'col'), may hold values from -120 to 120
- noise_var: float32 [8, 4, 8, 256], P(None, 'row', 'col'), may hold values from 2 to 4
- coords: float32 [3, 8, 4, 8, 256], P(None, None, 'row', 'col'), may hold values from 0 to 128
- tile_pairs: int32 [2, 4, 8, 64], P(None, 'row', 'col'), may hold values from 0 to 63, as said below
- tile_count: int32 [4, 8], P('row', 'col'), may hold values from 1 to 64, as said below
Outputs:
- new_solution: float32 [8, 8, 4, 8, 256], P(None, None, 'row', 'col')
- new_residual: float32 [8, 8, 4, 8, 256], P(None, None, 'row', 'col')
- new_direction: float32 [8, 8, 4, 8, 256], P(None, None, 'row', 'col')
Inputs may be any that keep to these rules, and one draw needn't show every extreme that they name: `tile_pairs`: entry [0, g, h, s] is one of the 64 row tiles of cell (g, h) and entry [1, g, h, s] one of its 32 column tiles; the first tile_count[g, h] pairs of a cell are distinct, and the mirror pair of each of them is live in the cell that holds it, so the kernel that the lists define is symmetric. `tile_count`: some cell holds exactly 64 live pairs.
All inputs are finite; a program needn't handle non-finite values.
Results may differ from a plain program's by a relative error of at most 0.0003.
Values sent between devices are 32-bit elements; how exact they have to be, the bound alone decides.
No kernel may reach another device: no remote copies, remote signals or barrier semaphores. Data moves between devices by JAX's collectives and lax.ppermute only.
A program may use at most 64 MiB of HBM per device.

v0:
```python
import jax
import jax.numpy as jnp
from jax import lax
from jax.sharding import PartitionSpec as P

EPS = 1e-06
KERNEL_SCALE = 0.125
HIGHEST = lax.Precision.HIGHEST


def wendland(target_pts, source_pts):
    delta_x = target_pts[0][:, None] - source_pts[0][None, :]
    delta_y = target_pts[1][:, None] - source_pts[1][None, :]
    delta_z = target_pts[2][:, None] - source_pts[2][None, :]
    distance = jnp.sqrt(delta_x * delta_x + delta_y * delta_y + delta_z * delta_z)
    reach_left = jnp.maximum(1.0 - distance, 0.0)
    squared = reach_left * reach_left
    return squared * squared * (4.0 * distance + 1.0)


def run_tiles(
    partial_value, start_slot, stop_slot, target_ids, source_ids, target_pts, source_pts, source_dir
):

    def add_tile(pair_slot, totals):
        target = target_ids[pair_slot]
        source = source_ids[pair_slot]
        kernel_block = wendland(
            lax.dynamic_index_in_dim(target_pts, target, 1, False),
            lax.dynamic_index_in_dim(source_pts, source, 1, False),
        )
        values = lax.dynamic_index_in_dim(source_dir, source, 1, False)
        contrib = jnp.dot(
            values, kernel_block.T, precision=HIGHEST, preferred_element_type=jnp.float32
        )
        current = lax.dynamic_index_in_dim(totals, target, 1, True)
        return lax.dynamic_update_index_in_dim(totals, current + contrib[:, None, :], target, 1)

    return lax.fori_loop(start_slot, stop_slot, add_tile, partial_value)


def per_device(solution, residual, direction, noise_var, coords, tile_pairs, tile_count):
    side_count, owned_tiles, _, _, tile_size = direction.shape
    pair_count = tile_count.reshape(())
    row_ids = tile_pairs[0].reshape(-1)
    col_ids = tile_pairs[1].reshape(-1)
    squares_now = jnp.sum(residual * residual, axis=(1, 2, 3, 4))
    norm_now = lax.psum(squares_now, ("row", "col"))
    row_pts = lax.all_gather(coords, "col", axis=3, tiled=True).reshape(3, -1, tile_size)
    col_pts, col_dir = (
        lax.all_gather(coords, "row", axis=2, tiled=True),
        lax.all_gather(direction, "row", axis=2, tiled=True),
    )
    col_pts = col_pts.reshape(3, -1, tile_size)
    col_dir = col_dir.reshape(side_count, -1, tile_size)
    partial_value = jnp.zeros((side_count, row_pts.shape[1], tile_size), jnp.float32)
    partial_value = run_tiles(
        partial_value, jnp.int32(0), pair_count, row_ids, col_ids, row_pts, col_pts, col_dir
    )
    folded = lax.psum_scatter(
        partial_value.reshape(side_count, owned_tiles, 1, -1, tile_size),
        "col",
        scatter_dimension=3,
        tiled=True,
    )
    applied = noise_var[None] * direction + KERNEL_SCALE * folded
    curvature = lax.psum(jnp.sum(direction * applied, axis=(1, 2, 3, 4)), ("row", "col"))
    step_size = (norm_now / curvature)[:, None, None, None, None]
    new_solution = solution + step_size * direction
    new_residual = residual - step_size * applied
    norm_next = lax.psum(jnp.sum(new_residual * new_residual, axis=(1, 2, 3, 4)), ("row", "col"))
    beta_ratio = (norm_next / (norm_now + EPS))[:, None, None, None, None]
    new_direction = new_residual + beta_ratio * direction
    return (new_solution, new_residual, new_direction)


def solution(mesh):
    in_specs = (
        P(None, None, "row", "col", None),
        P(None, None, "row", "col", None),
        P(None, None, "row", "col", None),
        P(None, "row", "col", None),
        P(None, None, "row", "col", None),
        P(None, "row", "col", None),
        P("row", "col"),
    )
    out_specs = (
        P(None, None, "row", "col", None),
        P(None, None, "row", "col", None),
        P(None, None, "row", "col", None),
    )
    return jax.shard_map(
        per_device, mesh=mesh, in_specs=in_specs, out_specs=out_specs, check_vma=False
    )
```

profile of v0, /device:TPU:0, one launch (start us, length us, event | category | flops | bytes accessed | tf_op | source)
XLA Modules:
  0.0 573.2 jit_solution(3877492613163081918)
XLA Ops:
  7.2 0.8 copy.22
  8.0 13.9 %all_gather.11 = f32[3,8,4,1,256]{4,3,2,1,0:T(1,128)S(1)} all-gather(f32[3,8,1,1,256]{4,3,2,1,0:T(1,128)S(1)} %copy-done.3), channel_id=1, replica_groups=mesh['row'=4,'col'=8] {'row'}, dimensions={2}, use_global_device_ids=true | all-gather | bytes 122880 | tf_op jit(solution)/shard_map/all_gather | solution.py:51
  21.9 9.8 %all_gather.9 = f32[8,8,4,1,256]{4,3,2,1,0:T(1,128)S(1)} all-gather(f32[8,8,1,1,256]{4,3,2,1,0:T(1,128)S(1)} %copy-done), channel_id=1, replica_groups=mesh['row'=4,'col'=8] {'row'}, dimensions={2}, use_global_device_ids=true | all-gather | bytes 327680 | tf_op jit(solution)/shard_map/all_gather | solution.py:52
  31.7 0.7 reduce
  32.5 9.3 %all_gather.10 = f32[3,8,1,8,256]{4,1,2,0,3:T(8,128)S(1)} all-gather(f32[3,8,1,1,256]{4,1,2,0,3:T(8,128)S(1)} %copy.22), channel_id=1, replica_groups=mesh['row'=4,'col'=8] {'col'}, dimensions={3}, use_global_device_ids=true | all-gather | bytes 221184 | tf_op jit(solution)/shard_map/all_gather | solution.py:49
  42.2 133.8 %while.10 = (s32[]{:T(128)}, f32[8,64,256]{2,0,1:T(8,128)S(1)}, s32[]{:T(128)}, s32[64]{0:T(128)S(1)}, s32[64]{0:T(128)S(1)}, /*index=5*/f32[8,32,256]{2,1,0:T(8...) while((s32[]{:T(128)}, f32[8,64,256]{2,0,1:T(8,128)S(1)}, ...), condition=%wide.region_3.4_spmd, body=%wide.region_2.3_spmd.sunk | while | flops 7276557 | bytes 59699 | solution.py:39
  42.9 0.6 dynamic_slice.31
  45.4 0.6 dynamic_slice.30
  49.2 0.6 dynamic_slice.31
  51.8 0.6 dynamic_slice.30
  55.6 0.6 dynamic_slice.31
  58.1 0.6 dynamic_slice.30
  61.9 0.6 dynamic_slice.31
  64.5 0.6 dynamic_slice.30
  68.3 0.6 dynamic_slice.31
  70.8 0.6 dynamic_slice.30
  74.6 0.6 dynamic_slice.31
  77.1 0.6 dynamic_slice.30
  80.9 0.6 dynamic_slice.31
  83.5 0.6 dynamic_slice.30
  87.3 0.6 dynamic_slice.31
  89.8 0.6 dynamic_slice.30
  93.6 0.6 dynamic_slice.31
  96.2 0.6 dynamic_slice.30
  100.0 0.6 dynamic_slice.31
  102.5 0.6 dynamic_slice.30
  106.3 0.6 dynamic_slice.31
  108.8 0.6 dynamic_slice.30
  115.2 0.6 dynamic_slice.30
  119.0 0.6 dynamic_slice.31
  121.5 0.6 dynamic_slice.30
  127.9 0.6 dynamic_slice.30
  134.2 0.6 dynamic_slice.30
  140.5 0.6 dynamic_slice.30
  146.9 0.6 dynamic_slice.30
  153.2 0.6 dynamic_slice.30
  159.5 0.6 dynamic_slice.30
  165.9 0.6 dynamic_slice.30
  172.2 0.6 dynamic_slice.30
  176.0 1.1 copy.25
  177.2 0.7 copy-done.5
  178.1 304.4 %reduce-scatter.2.cloned.1.call-done = f32[8,8,1,1,256]{4,1,2,0,3:T(8,128)} async-done(((f32[8,8,1,8,256]{4,1,2,0,3:T(8,128)}), f32[8,8,1,1,256]{4,1,2,0,3:T(8,128)}) %reduce-scatter.2.cloned.1.call-update) | async-done | bytes 65552 | tf_op jit(solution)/shard_map/reduce_scatter | solution.py:60
  482.6 1.1 multiply_reduce_fusion.1
  483.6 39.3 %all-reduce = (f32[8]{0:T(128)S(1)}, f32[8]{0:T(128)S(1)}) all-reduce(f32[8]{0:T(128)S(1)} %multiply_reduce_fusion.2, f32[8]{0:T(128)S(1)} %multiply_reduce_fusion.1), channel_id=1, replica_groups=mesh['row'=4,'col'=8] {'row','col'}, use_global_device_ids=true, to_apply=%region_1.0 | all-reduce | flops 16 | bytes 128 | tf_op jit(solution)/shard_map/psum | solution.py:48
  523.2 41.0 %psum.23 = f32[8]{0:T(128)S(1)} all-reduce(f32[8]{0:T(128)S(1)} %get-tuple-element.71), channel_id=1, replica_groups=mesh['row'=4,'col'=8] {'row','col'}, use_global_device_ids=true, to_apply=%region_8.9 | all-reduce | flops 8 | bytes 64 | tf_op jit(solution)/shard_map/psum | solution.py:71
  564.2 0.7 copy.32
  564.9 0.7 copy.33
  565.6 0.7 copy.31
  (99 shorter events, 17.5 us)
Async XLA Ops:
  7.2 0.8 copy-start.3
  7.2 475.4 %reduce-scatter.2.cloned.1.call-start = ((), (), s32[]{:S(2)}) async-start(), calls=%async_computation.1 | async-start | bytes 589824 | tf_op jit(solution)/shard_map/reduce_scatter | solution.py:60
  8.0 13.9 %copy-start.6 = (s32[2,1,1,64]{3,2,1,0:T(1,128)S(1)}, s32[2,1,1,64]{3,2,1,0:T(1,128)}, u32[]{:S(2)}) copy-start(s32[2,1,1,64]{3,2,1,0:T(1,128)} %param.14) | copy-start | bytes 1540
  8.0 13.9 %copy-start = (f32[8,8,1,1,256]{4,3,2,1,0:T(1,128)S(1)}, f32[8,8,1,1,256]{4,3,2,1,0:T(1,128)}, u32[]{:S(2)}) copy-start(f32[8,8,1,1,256]{4,3,2,1,0:T(1,128)} %param.11) | copy-start | bytes 196612
  177.1 0.7 copy-start.5
  177.1 0.9 copy-start.1
  482.6 40.4 %copy-start.2 = (f32[8,8,1,1,256]{4,1,2,0,3:T(8,128)S(1)}, f32[8,8,1,1,256]{4,1,2,0,3:T(8,128)}, u32[]{:S(2)}) copy-start(f32[8,8,1,1,256]{4,1,2,0,3:T(8,128)} %reduce-scatter.2.cloned.1.call-done) | copy-start | bytes 196612
  482.6 40.4 %copy-start.4 = (f32[8,8,1,1,256]{4,3,2,1,0:T(1,128)S(1)}, f32[8,8,1,1,256]{4,3,2,1,0:T(1,128)}, u32[]{:S(2)}) copy-start(f32[8,8,1,1,256]{4,3,2,1,0:T(1,128)} %param.9) | copy-start | bytes 196612
Sparse Core Ops, SparseCore 0:
  177.3 305.2 reduce-scatter.1
where the time goes:
time: 582 us; the launch traced here: 573 us
  waiting for transfers between devices  304 us (52%)
  blocking collectives  113 us (19%)
  loops' own time  98.1 us (17%)
  local copies, waits for them, and re-layouts  30.5 us (5%)
  between operations  14.1 us (2%)
  matrix products  10.2 us (2%)
    reduce_scatter x1, waiting for transfers between devices, per_device(): lax.psum_scatter(partial_value.reshape(side_count, owned_tiles, 1, -1, ti...  304 us
    another operation x1, loops' own time, run_tiles(): return lax.fori_loop(start_slot, stop_slot, add_tile, partial_value)  98.1 us
    psum x1, blocking collectives, per_device(): lax.psum(jnp.sum(new_residual * new_residual, axis=(1, 2, 3, 4)), ('row',...  41 us
    psum x1, blocking collectives, per_device(): norm_now = lax.psum(squares_now, ('row', 'col'))  39.3 us
    all_gather x1, blocking collectives, per_device(): lax.all_gather(coords, 'row', axis=2, tiled=True)  13.9 us
    dynamic_slice x21, local copies, waits for them, and re-layouts, add_tile(): target = target_ids[pair_slot]  12.4 us
    dynamic_slice x21, local copies, waits for them, and re-layouts, add_tile(): source = source_ids[pair_slot]  12.3 us
  transfers between devices with their start and end apart: 1, of which 1 were waited for; matrix products, arithmetic and copies ran while one was open for 0% of the time, Pallas kernels for 0%

commit v1 on v0

v1 whole, which is shorter than its diff:
```python
import functools
import jax
import jax.numpy as jnp
from jax import lax
from jax.experimental import pallas as pl
from jax.experimental.pallas import tpu as pltpu
from jax.sharding import PartitionSpec as P

EPS = 1e-06
SCALED_KERNEL = 0.125 / 256.0
TINY = 1e-30
LANES = 128
SLAB = 256


def pair_kernel(rows, cols, owned, count_ref, pairs_ref, *refs):
    sources = refs[:cols]
    targets = refs[cols : cols + rows]
    outs = refs[cols + rows : cols + 2 * rows]
    slab, spots, totals = refs[cols + 2 * rows :]
    my_row = lax.axis_index("row")
    my_col = lax.axis_index("col")
    spread = sources[0].shape[0]
    for shift in range(cols):
        slab[lax.rem(my_col - shift + cols, cols), pl.ds(0, spread), :] = sources[shift][...]
    for shift in range(rows):
        spots[lax.rem(my_row - shift + rows, rows)] = 4.0 * targets[shift][...]
    totals[...] = jnp.zeros_like(totals)
    sides = 8
    stride = 2 * owned
    held = sides * stride

    def add_pair(slot, carry):
        row_tile = pairs_ref[0, slot]
        col_tile = pairs_ref[1, slot]
        origin = lax.rem(row_tile, cols)
        lane_row = 2 * lax.div(row_tile, cols)
        owner = lax.rem(col_tile, rows)
        spot_row = 2 * lax.div(col_tile, rows)
        spot = [
            [spots[owner, pl.ds(axis * stride + spot_row + half, 1), :] for axis in range(3)]
            for half in range(2)
        ]
        high_parts, low_parts, lhs_parts = [], [], []
        for side in range(2):
            values = slab[origin, pl.ds(lane_row + side, sides, stride=stride), :]
            lead = values.astype(jnp.bfloat16)
            rest = (values - lead.astype(jnp.float32)).astype(jnp.bfloat16)
            lhs_parts.append(jnp.concatenate([lead, rest], axis=0))
            points = 4.0 * slab[origin, pl.ds(held + lane_row + side, sides, stride=stride), :]
            turned = jnp.transpose(points)
            for step in range(LANES // 16):
                part = turned[16 * step : 16 * step + 16]
                grid = [jnp.broadcast_to(part[:, axis : axis + 1], (16, LANES)) for axis in range(3)]
                halves_high, halves_low = [], []
                for half in range(2):
                    dx = grid[0] - spot[half][0]
                    dy = grid[1] - spot[half][1]
                    dz = grid[2] - spot[half][2]
                    square = dx * dx + dy * dy + dz * dz
                    distance = square * lax.rsqrt(jnp.maximum(square, TINY))
                    left = jnp.maximum(4.0 - distance, 0.0)
                    left = left * left
                    weight = left * left * (distance + 1.0)
                    high = weight.astype(jnp.bfloat16)
                    halves_high.append(high)
                    halves_low.append((weight - high.astype(jnp.float32)).astype(jnp.bfloat16))
                high_parts.append(jnp.concatenate(halves_high, axis=1))
                low_parts.append(jnp.concatenate(halves_low, axis=1))
        lhs = jnp.concatenate(lhs_parts, axis=1)
        product = jnp.dot(
            lhs, jnp.concatenate(high_parts, axis=0), preferred_element_type=jnp.float32
        ) + jnp.dot(lhs, jnp.concatenate(low_parts, axis=0), preferred_element_type=jnp.float32)
        summed = product[:sides] + product[sides:]
        for half in range(2):
            totals[owner, spot_row + half] += summed[:, LANES * half : LANES * half + LANES]
        return carry

    lax.fori_loop(0, count_ref[0, 0], add_pair, jnp.int32(0))
    for shift in range(rows):
        outs[shift][...] = totals[lax.rem(my_row + shift, rows)]


def sums_kernel(rows, parts, residual_ref, direction_ref, noise_ref, *refs):
    partials = refs[:rows]
    applied_ref, stats_ref, stack = refs[rows:]
    halves = noise_ref.shape[0]
    sides = residual_ref.shape[0] // halves
    zero = jnp.zeros((sides, LANES), jnp.float32)
    now, bend, cross, size = zero, zero, zero, zero
    for part in range(halves):
        total = partials[0][part]
        for other in partials[1:]:
            total = total + other[part]
        residual = residual_ref[pl.ds(part, sides, stride=halves), :]
        direction = direction_ref[pl.ds(part, sides, stride=halves), :]
        applied = noise_ref[part : part + 1, :] * direction + SCALED_KERNEL * total
        applied_ref[part] = applied
        now = now + residual * residual
        bend = bend + direction * applied
        cross = cross + residual * applied
        size = size + applied * applied
    stack[...] = jnp.zeros_like(stack)
    for slot, value in enumerate((now, bend, cross, size)):
        stack[sides * slot : sides * slot + sides, :] = value
    stats_ref[...] = lax.dot_general(
        jnp.ones((parts, LANES), jnp.float32),
        stack[...],
        (((1,), (1,)), ((), ())),
        precision=lax.Precision.HIGHEST,
        preferred_element_type=jnp.float32,
    )


def step_kernel(
    stats_ref, applied_ref, solution_ref, residual_ref, direction_ref, new_x, new_r, new_d
):
    halves = applied_ref.shape[0]
    sides = applied_ref.shape[1]
    summed = jnp.sum(stats_ref[...], axis=0, keepdims=True)
    summed = jnp.broadcast_to(summed, (sides, LANES))
    lane = lax.broadcasted_iota(jnp.int32, (sides, LANES), 1)
    line = lax.broadcasted_iota(jnp.int32, (sides, LANES), 0)

    def pick(slot):
        return jnp.sum(
            jnp.where(lane == line + sides * slot, summed, 0.0), axis=1, keepdims=True
        )

    now, bend, cross, size = pick(0), pick(1), pick(2), pick(3)
    step = now / bend
    after = jnp.maximum(now - 2.0 * step * cross + step * step * size, 0.0)
    beta = jnp.broadcast_to(after / (now + EPS), (sides, LANES))
    step = jnp.broadcast_to(step, (sides, LANES))
    for part in range(halves):
        place = pl.ds(part, sides, stride=halves)
        direction = direction_ref[place, :]
        new_x[place, :] = solution_ref[place, :] + step * direction
        residual = residual_ref[place, :] - step * applied_ref[part]
        new_r[place, :] = residual
        new_d[place, :] = residual + beta * direction


def per_device(rows, cols, solution, residual, direction, noise_var, coords, tile_pairs, tile_count):
    sides, owned, _, _, tile_size = direction.shape
    parts = rows * cols
    halves = owned * tile_size // LANES
    flat_x = solution.reshape(-1, LANES)
    flat_r = residual.reshape(-1, LANES)
    flat_d = direction.reshape(-1, LANES)
    flat_c = coords.reshape(-1, LANES)
    mine = jnp.concatenate([flat_d, flat_c], axis=0)
    sources = [mine] + [
        lax.ppermute(mine, "col", [(at, (at + shift) % cols) for at in range(cols)])
        for shift in range(1, cols)
    ]
    targets = [flat_c] + [
        lax.ppermute(flat_c, "row", [(at, (at + shift) % rows) for at in range(rows)])
        for shift in range(1, rows)
    ]
    vmem = pl.BlockSpec(memory_space=pltpu.VMEM)
    smem = pl.BlockSpec(memory_space=pltpu.SMEM)
    block = jax.ShapeDtypeStruct((halves, sides, LANES), jnp.float32)
    flat = jax.ShapeDtypeStruct(flat_d.shape, jnp.float32)
    partials = pl.pallas_call(
        functools.partial(pair_kernel, rows, cols, owned),
        out_shape=[block] * rows,
        in_specs=[smem, smem] + [vmem] * (cols + rows),
        out_specs=[vmem] * rows,
        scratch_shapes=[
            pltpu.VMEM((cols, SLAB, LANES), jnp.float32),
            pltpu.VMEM((rows,) + flat_c.shape, jnp.float32),
            pltpu.VMEM((rows, halves, sides, LANES), jnp.float32),
        ],
        compiler_params=pltpu.CompilerParams(vmem_limit_bytes=32 << 20),
        name="pairs",
    )(tile_count, tile_pairs.reshape(2, -1), *sources, *targets)
    partials = [partials[0]] + [
        lax.ppermute(partials[shift], "row", [(at, (at + shift) % rows) for at in range(rows)])
        for shift in range(1, rows)
    ]
    applied, stats = pl.pallas_call(
        functools.partial(sums_kernel, rows, parts),
        out_shape=[block, jax.ShapeDtypeStruct((parts, LANES), jnp.float32)],
        in_specs=[vmem] * (3 + rows),
        out_specs=[vmem] * 2,
        scratch_shapes=[pltpu.VMEM((LANES, LANES), jnp.float32)],
        name="sums",
    )(flat_r, flat_d, noise_var.reshape(-1, LANES), *partials)
    stats = lax.all_to_all(stats, ("row", "col"), 0, 0, tiled=True)
    new_x, new_r, new_d = pl.pallas_call(
        step_kernel,
        out_shape=[flat] * 3,
        in_specs=[vmem] * 5,
        out_specs=[vmem] * 3,
        name="step",
    )(stats, applied, flat_x, flat_r, flat_d)
    return tuple(new.reshape(direction.shape) for new in (new_x, new_r, new_d))


def solution(mesh):
    field = P(None, None, "row", "col", None)
    in_specs = (field, field, field, P(None, "row", "col", None), field, P(None, "row", "col", None), P("row", "col"))
    return jax.shard_map(
        functools.partial(per_device, mesh.shape["row"], mesh.shape["col"]),
        mesh=mesh,
        in_specs=in_specs,
        out_specs=(field, field, field),
        check_vma=False,
    )
```

time: 582 us -> 74.8 us (0.13); the launches traced: 573 us -> 74.5 us
  waiting for transfers between devices: 304 us -> 11.5 us
  blocking collectives: 113 us -> 11.8 us
  loops' own time: 98.1 us -> 0 us
  starting transfers between devices: 0.04 us -> 32.7 us
  local copies, waits for them, and re-layouts: 30.5 us -> 1.26 us
  Pallas kernels: 0 us -> 15 us
  between operations: 14.1 us -> 1.35 us
  matrix products: 10.2 us -> 0 us
    reduce_scatter x1 -> x0, waiting for transfers between devices: 304 us -> none  [per_device(): lax.psum_scatter(partial_value.reshape(side_count, owned_tiles, 1, -1, ti...]
    another operation x1 -> x0, loops' own time: 98.1 us -> none  [run_tiles(): return lax.fori_loop(start_slot, stop_slot, add_tile, partial_value)]
    psum x2 -> x0, blocking collectives: 80.3 us -> none  [the longest x1 41 us: per_device(): lax.psum(jnp.sum(new_residual * new_residual, axis=(1, 2, 3, 4)), ('row',...]
    all_gather x3 -> x0, blocking collectives: 33 us -> none  [the longest x1 13.9 us: per_device(): lax.all_gather(coords, 'row', axis=2, tiled=True)]
    ppermute x0 -> x13, starting transfers between devices: none -> 32.7 us  [the longest x3 21.3 us: per_device(): lax.ppermute(partials[shift], 'row', [(at, (at + shift) % rows) for at in...]
    dynamic_slice x63 -> x0, local copies, waits for them, and re-layouts: 25 us -> none  [the longest x21 12.4 us: add_tile(): target = target_ids[pair_slot]]
    pallas_call x0 -> x3, Pallas kernels: none -> 15 us  [the longest x1 11.4 us: per_device(): pl.pallas_call(functools.partial(pair_kernel, rows, cols, owned), out_sha...]
    all_to_all x0 -> x1, blocking collectives: none -> 11.8 us  [per_device(): stats = lax.all_to_all(stats, ('row', 'col'), 0, 0, tiled=True)]
  transfers between devices with their start and end apart: 1 -> 13, of which waited for: 1 -> 6; matrix products, arithmetic and copies ran while one was open for 0% -> 0% of each run, Pallas kernels for 0% -> 0%
where the time goes in v1:
time: 74.8 us; the launch traced here: 74.5 us
  starting transfers between devices  32.7 us (44%)
  Pallas kernels  15 us (20%)
  blocking collectives  11.8 us (16%)
  waiting for transfers between devices  11.5 us (15%)
  between operations  1.35 us (2%)
  local copies, waits for them, and re-layouts  1.26 us (2%)
  other arithmetic  0.87 us (1%)
    ppermute x3, starting transfers between devices, per_device(): lax.ppermute(partials[shift], 'row', [(at, (at + shift) % rows) for at in...  21.3 us
    all_to_all x1, blocking collectives, per_device(): stats = lax.all_to_all(stats, ('row', 'col'), 0, 0, tiled=True)  11.8 us
    pallas_call x1, Pallas kernels, per_device(): pl.pallas_call(functools.partial(pair_kernel, rows, cols, owned), out_sha...  11.4 us
    ppermute x7, starting transfers between devices, per_device(): lax.ppermute(mine, 'col', [(at, (at + shift) % cols) for at in range(cols)])  6.83 us
    ppermute x7, waiting for transfers between devices, per_device(): lax.ppermute(mine, 'col', [(at, (at + shift) % cols) for at in range(cols)])  5.5 us
    ppermute x3, starting transfers between devices, per_device(): lax.ppermute(flat_c, 'row', [(at, (at + shift) % rows) for at in range(ro...  4.62 us
    ppermute x3, waiting for transfers between devices, per_device(): lax.ppermute(flat_c, 'row', [(at, (at + shift) % rows) for at in range(ro...  4.1 us
    ppermute x3, waiting for transfers between devices, per_device(): lax.ppermute(partials[shift], 'row', [(at, (at + shift) % rows) for at in...  1.89 us
  transfers between devices with their start and end apart: 13, of which 6 were waited for; matrix products, arithmetic and copies ran while one was open for 0% of the time, Pallas kernels for 0%

profile of v1, /device:TPU:0, one launch (start us, length us, event | category | flops | bytes accessed | tf_op | source)
XLA Modules:
  0.0 74.5 jit_solution(12210015154903794221)
XLA Ops:
  0.6 0.0 copy-start
  0.6 0.9 %pad_maximum_fusion.refs_0_ = f32[176,128]{1,0:T(8,128)S(1)} fusion(f32[48,128]{1,0:T(8,128)} %bitcast.13, f32[128,128]{1,0:T(8,128)} %bitcast.19), kind=kLoop, calls=%fused_computation | loop fusion | flops 22528 | bytes 180224 | tf_op jit(solution)/shard_map/concatenate | solution.py:152
  1.5 3.3 %collective-permute-start.6 = (f32[176,128]{1,0:T(8,128)S(1)}, f32[176,128]{1,0:T(8,128)S(1)}, u32[]{:S(2)}, u32[]{:S(2)}) collective-permute-start(f32[176,128]{1,0:T(8,128)S(1)} %pad_maximum_fusion.refs_0_), channel_id=1, source_target_pairs={{0,7},{1,0},{2,1},{3,2},{4,3},{5,4},{6,5},{7,6},{8,15},{9,8},{10,9... | collective-permute-start | bytes 270344 | tf_op jit(solution)/shard_map/ppermute | solution.py:154
  4.8 0.6 collective-permute-start.5
  5.5 0.0 copy-done
  5.5 3.6 %collective-permute-start.9 = (f32[48,128]{1,0:T(8,128)S(1)}, f32[48,128]{1,0:T(8,128)S(1)}, u32[]{:S(2)}, u32[]{:S(2)}) collective-permute-start(f32[48,128]{1,0:T(8,128)S(1)} %bitcast.14), channel_id=1, source_target_pairs={{0,24},{8,0},{16,8},{24,16},{1,25},{9,1},{17,9},{25,17},{2,26},{10... | collective-permute-start | bytes 73736 | tf_op jit(solution)/shard_map/ppermute | solution.py:158
  9.1 0.0 collective-permute-start.8
  9.1 1.0 %collective-permute-start.7 = (f32[48,128]{1,0:T(8,128)S(1)}, f32[48,128]{1,0:T(8,128)S(1)}, u32[]{:S(2)}, u32[]{:S(2)}) collective-permute-start(f32[48,128]{1,0:T(8,128)S(1)} %bitcast.16), channel_id=1, source_target_pairs={{0,8},{8,16},{16,24},{24,0},{1,9},{9,17},{17,25},{25,1},{2,10},{10... | collective-permute-start | bytes 73736 | tf_op jit(solution)/shard_map/ppermute | solution.py:158
  10.1 0.5 collective-permute-done.9.refs_11_
  10.6 0.0 collective-permute-start.4
  10.6 3.3 %collective-permute-done.8.refs_10_ = f32[48,128]{1,0:T(8,128)S(1)} collective-permute-done((f32[48,128]{1,0:T(8,128)S(1)}, f32[48,128]{1,0:T(8,128)S(1)}, u32[]{:S(2)}, u32[]{:S(2)}) %collective-permute-start.8) | collective-permute-done | bytes 24608 | tf_op jit(solution)/shard_map/ppermute | solution.py:158
  13.9 0.5 collective-permute-start.3
  14.4 0.3 collective-permute-done.7.refs_9_
  14.7 0.0 collective-permute-start.2
  14.7 0.0 collective-permute-done.6.refs_7_
  14.7 1.4 %collective-permute-start.1 = (f32[176,128]{1,0:T(8,128)S(1)}, f32[176,128]{1,0:T(8,128)S(1)}, u32[]{:S(2)}, u32[]{:S(2)}) collective-permute-start(f32[176,128]{1,0:T(8,128)S(1)} %pad_maximum_fusion.refs_0_), channel_id=1, source_target_pairs={{0,2},{1,3},{2,4},{3,5},{4,6},{5,7},{6,0},{7,1},{8,10},{9,11},{10,... | collective-permute-start | bytes 270344 | tf_op jit(solution)/shard_map/ppermute | solution.py:154
  16.1 0.0 collective-permute-done.5.refs_6_
  16.1 1.0 %collective-permute-start = (f32[176,128]{1,0:T(8,128)S(1)}, f32[176,128]{1,0:T(8,128)S(1)}, u32[]{:S(2)}, u32[]{:S(2)}) collective-permute-start(f32[176,128]{1,0:T(8,128)S(1)} %pad_maximum_fusion.refs_0_), channel_id=1, source_target_pairs={{0,1},{1,2},{2,3},{3,4},{4,5},{5,6},{6,7},{7,0},{8,9},{9,10},{10,1... | collective-permute-start | bytes 270344 | tf_op jit(solution)/shard_map/ppermute | solution.py:154
  17.7 0.0 copy-start.2
  17.7 0.0 collective-permute-done.4.refs_5_
  17.7 5.2 %collective-permute-done.3.refs_4_ = f32[176,128]{1,0:T(8,128)S(1)} collective-permute-done((f32[176,128]{1,0:T(8,128)S(1)}, f32[176,128]{1,0:T(8,128)S(1)}, u32[]{:S(2)}, u32[]{:S(2)}) %collective-permute-start.3) | collective-permute-done | bytes 90144 | tf_op jit(solution)/shard_map/ppermute | solution.py:154
  23.0 0.2 collective-permute-done.2.refs_3_
  23.2 0.0 collective-permute-done.1.refs_2_
  23.2 0.0 collective-permute-done.refs_1_
  23.2 0.0 copy-done.2
  23.3 11.4 %pairs.1 = (f32[16,8,128]{2,1,0:T(8,128)S(1)}, f32[16,8,128]{2,1,0:T(8,128)S(1)}, f32[16,8,128]{2,1,0:T(8,128)S(1)}, f32[16,8,128]{2,1,0:T(8,128)S(1)}) custom-call(s32[1,1]{1,0:T(1,128)S(6)} %copy.17.count_ref, s32[2,64]{1,0:T(2,128)S(1)} %bitcast.18, f32[176,128]{1,0:T(8,128)S(1)} %pad_maximum_fusion.refs_0_, f32[176,128]{1,0:T(8,128)S(1)} %collective-permute-done.refs_1_, ...), custom_call_target="tpu_custom_call" | custom-call | tf_op jit(solution)/shard_map/pairs/pallas_call | solution.py:165
  34.7 0.0 copy-start.1
  34.7 0.6 copy-done.1
  35.3 2.0 %collective-permute-start.10 = (f32[16,8,128]{2,1,0:T(8,128)S(1)}, f32[16,8,128]{2,1,0:T(8,128)S(1)}, u32[]{:S(2)}, u32[]{:S(2)}) collective-permute-start(f32[16,8,128]{2,1,0:T(8,128)S(1)} %get-tuple-element.13), channel_id=1, source_target_pairs={{0,8},{8,16},{16,24},{24,0},{1,9},{9,17},{17,25},{25,1},{2,10},{10... | collective-permute-start | bytes 196616 | tf_op jit(solution)/shard_map/ppermute | solution.py:179
  37.3 16.4 %collective-permute-start.11 = (f32[16,8,128]{2,1,0:T(8,128)S(1)}, f32[16,8,128]{2,1,0:T(8,128)S(1)}, u32[]{:S(2)}, u32[]{:S(2)}) collective-permute-start(f32[16,8,128]{2,1,0:T(8,128)S(1)} %get-tuple-element.14), channel_id=1, source_target_pairs={{0,16},{8,24},{16,0},{24,8},{1,17},{9,25},{17,1},{25,9},{2,18},{10... | collective-permute-start | bytes 196616 | tf_op jit(solution)/shard_map/ppermute | solution.py:179
  53.7 2.9 %collective-permute-start.12 = (f32[16,8,128]{2,1,0:T(8,128)S(1)}, f32[16,8,128]{2,1,0:T(8,128)S(1)}, u32[]{:S(2)}, u32[]{:S(2)}) collective-permute-start(f32[16,8,128]{2,1,0:T(8,128)S(1)} %get-tuple-element.15), channel_id=1, source_target_pairs={{0,24},{8,0},{16,8},{24,16},{1,25},{9,1},{17,9},{25,17},{2,26},{10... | collective-permute-start | bytes 196616 | tf_op jit(solution)/shard_map/ppermute | solution.py:179
  56.6 0.0 collective-permute-done.10.refs_1_
  56.6 0.0 copy-start.3
  56.6 0.0 collective-permute-done.11.refs_2_
  56.6 0.0 copy-start.4
  56.6 1.9 %collective-permute-done.12.refs_3_ = f32[16,8,128]{2,1,0:T(8,128)S(1)} collective-permute-done((f32[16,8,128]{2,1,0:T(8,128)S(1)}, f32[16,8,128]{2,1,0:T(8,128)S(1)}, u32[]{:S(2)}, u32[]{:S(2)}) %collective-permute-start.12) | collective-permute-done | bytes 65568 | tf_op jit(solution)/shard_map/ppermute | solution.py:179
  58.5 0.0 copy-start.5
  58.5 0.0 copy-done.3
  58.5 0.0 copy-done.4
  58.5 0.6 copy-done.5
  59.1 1.8 %sums.1 = (f32[16,8,128]{2,1,0:T(8,128)}, f32[32,128]{1,0:T(8,128)}) custom-call(f32[128,128]{1,0:T(8,128)} %bitcast.22, f32[128,128]{1,0:T(8,128)} %bitcast.20, f32[16,128]{1,0:T(8,128)} %bitcast.27, f32[16,8,128]{2,1,0:T(8,128)} %copy-done.1, f32[16,8,128]{2,1,0:T(8,128)} %copy-done.3, f32[16,8,128]{2,1,0:T(8,128)} %copy-done.4, f32[16,8,128]{2,1,0:T(8,128)} %copy-done.5), custom_call_target="tpu_custom_call" | custom-call | tf_op jit(solution)/shard_map/sums/pallas_call | solution.py:182
  60.9 11.8 %all_to_all.11 = f32[32,1,128]{2,1,0:T(1,128)} all-to-all(f32[32,1,128]{2,1,0:T(1,128)} %bitcast.26), channel_id=1, replica_groups=mesh['row'=4,'col'=8] {'row','col'}, dimensions={0} | all-to-all | bytes 32768 | tf_op jit(solution)/shard_map/all_to_all | solution.py:190
  72.7 1.8 %step.1 = (f32[128,128]{1,0:T(8,128)}, f32[128,128]{1,0:T(8,128)}, f32[128,128]{1,0:T(8,128)}) custom-call(f32[32,128]{1,0:T(8,128)} %bitcast.25, f32[16,8,128]{2,1,0:T(8,128)} %get-tuple-element.17.applied_ref, f32[128,128]{1,0:T(8,128)} %bitcast.24, f32[128,128]{1,0:T(8,128)} %bitcast.23, f32[128,128]{1,0:T(8,128)} %bitcast.21), custom_call_target="tpu_custom_call" | custom-call | tf_op jit(solution)/shard_map/step/pallas_call | solution.py:191
Async XLA Ops:
  0.6 4.8 %copy-start = (f32[3,8,1,1,256]{4,3,2,1,0:T(1,128)S(1)}, f32[3,8,1,1,256]{4,3,2,1,0:T(1,128)}, u32[]{:S(2)}) copy-start(f32[3,8,1,1,256]{4,3,2,1,0:T(1,128)} %param.11) | copy-start | bytes 73732
  1.5 13.2 %collective-permute-start.6 = (f32[176,128]{1,0:T(8,128)S(1)}, f32[176,128]{1,0:T(8,128)S(1)}, u32[]{:S(2)}, u32[]{:S(2)}) collective-permute-start(f32[176,128]{1,0:T(8,128)S(1)} %pad_maximum_fusion.refs_0_), channel_id=1, source_target_pairs={{0,7},{1,0},{2,1},{3,2},{4,3},{5,4},{6,5},{7,6},{8,15},{9,8},{10,9... | collective-permute-start | bytes 270344 | tf_op jit(solution)/shard_map/ppermute | solution.py:154
  4.8 11.3 %collective-permute-start.5 = (f32[176,128]{1,0:T(8,128)S(1)}, f32[176,128]{1,0:T(8,128)S(1)}, u32[]{:S(2)}, u32[]{:S(2)}) collective-permute-start(f32[176,128]{1,0:T(8,128)S(1)} %pad_maximum_fusion.refs_0_), channel_id=1, source_target_pairs={{0,6},{1,7},{2,0},{3,1},{4,2},{5,3},{6,4},{7,5},{8,14},{9,15},{10,... | collective-permute-start | bytes 270344 | tf_op jit(solution)/shard_map/ppermute | solution.py:154
  5.5 5.1 %collective-permute-start.9 = (f32[48,128]{1,0:T(8,128)S(1)}, f32[48,128]{1,0:T(8,128)S(1)}, u32[]{:S(2)}, u32[]{:S(2)}) collective-permute-start(f32[48,128]{1,0:T(8,128)S(1)} %bitcast.14), channel_id=1, source_target_pairs={{0,24},{8,0},{16,8},{24,16},{1,25},{9,1},{17,9},{25,17},{2,26},{10... | collective-permute-start | bytes 73736 | tf_op jit(solution)/shard_map/ppermute | solution.py:158
  9.1 4.8 %collective-permute-start.8 = (f32[48,128]{1,0:T(8,128)S(1)}, f32[48,128]{1,0:T(8,128)S(1)}, u32[]{:S(2)}, u32[]{:S(2)}) collective-permute-start(f32[48,128]{1,0:T(8,128)S(1)} %bitcast.15), channel_id=1, source_target_pairs={{0,16},{8,24},{16,0},{24,8},{1,17},{9,25},{17,1},{25,9},{2,18},{10... | collective-permute-start | bytes 73736 | tf_op jit(solution)/shard_map/ppermute | solution.py:158
  9.1 5.6 %collective-permute-start.7 = (f32[48,128]{1,0:T(8,128)S(1)}, f32[48,128]{1,0:T(8,128)S(1)}, u32[]{:S(2)}, u32[]{:S(2)}) collective-permute-start(f32[48,128]{1,0:T(8,128)S(1)} %bitcast.16), channel_id=1, source_target_pairs={{0,8},{8,16},{16,24},{24,0},{1,9},{9,17},{17,25},{25,1},{2,10},{10... | collective-permute-start | bytes 73736 | tf_op jit(solution)/shard_map/ppermute | solution.py:158
  10.6 7.1 %collective-permute-start.4 = (f32[176,128]{1,0:T(8,128)S(1)}, f32[176,128]{1,0:T(8,128)S(1)}, u32[]{:S(2)}, u32[]{:S(2)}) collective-permute-start(f32[176,128]{1,0:T(8,128)S(1)} %pad_maximum_fusion.refs_0_), channel_id=1, source_target_pairs={{0,5},{1,6},{2,7},{3,0},{4,1},{5,2},{6,3},{7,4},{8,13},{9,14},{10,... | collective-permute-start | bytes 270344 | tf_op jit(solution)/shard_map/ppermute | solution.py:154
  13.9 9.1 %collective-permute-start.3 = (f32[176,128]{1,0:T(8,128)S(1)}, f32[176,128]{1,0:T(8,128)S(1)}, u32[]{:S(2)}, u32[]{:S(2)}) collective-permute-start(f32[176,128]{1,0:T(8,128)S(1)} %pad_maximum_fusion.refs_0_), channel_id=1, source_target_pairs={{0,4},{1,5},{2,6},{3,7},{4,0},{5,1},{6,2},{7,3},{8,12},{9,13},{10,... | collective-permute-start | bytes 270344 | tf_op jit(solution)/shard_map/ppermute | solution.py:154
  14.7 8.5 %collective-permute-start.2 = (f32[176,128]{1,0:T(8,128)S(1)}, f32[176,128]{1,0:T(8,128)S(1)}, u32[]{:S(2)}, u32[]{:S(2)}) collective-permute-start(f32[176,128]{1,0:T(8,128)S(1)} %pad_maximum_fusion.refs_0_), channel_id=1, source_target_pairs={{0,3},{1,4},{2,5},{3,6},{4,7},{5,0},{6,1},{7,2},{8,11},{9,12},{10,... | collective-permute-start | bytes 270344 | tf_op jit(solution)/shard_map/ppermute | solution.py:154
  14.7 8.5 %collective-permute-start.1 = (f32[176,128]{1,0:T(8,128)S(1)}, f32[176,128]{1,0:T(8,128)S(1)}, u32[]{:S(2)}, u32[]{:S(2)}) collective-permute-start(f32[176,128]{1,0:T(8,128)S(1)} %pad_maximum_fusion.refs_0_), channel_id=1, source_target_pairs={{0,2},{1,3},{2,4},{3,5},{4,6},{5,7},{6,0},{7,1},{8,10},{9,11},{10,... | collective-permute-start | bytes 270344 | tf_op jit(solution)/shard_map/ppermute | solution.py:154
  16.1 7.1 %collective-permute-start = (f32[176,128]{1,0:T(8,128)S(1)}, f32[176,128]{1,0:T(8,128)S(1)}, u32[]{:S(2)}, u32[]{:S(2)}) collective-permute-start(f32[176,128]{1,0:T(8,128)S(1)} %pad_maximum_fusion.refs_0_), channel_id=1, source_target_pairs={{0,1},{1,2},{2,3},{3,4},{4,5},{5,6},{6,7},{7,0},{8,9},{9,10},{10,1... | collective-permute-start | bytes 270344 | tf_op jit(solution)/shard_map/ppermute | solution.py:154
  17.7 5.5 %copy-start.2 = (s32[2,1,1,64]{3,2,1,0:T(1,128)S(1)}, s32[2,1,1,64]{3,2,1,0:T(1,128)}, u32[]{:S(2)}) copy-start(s32[2,1,1,64]{3,2,1,0:T(1,128)} %param.12) | copy-start | bytes 1540
  34.7 0.6 copy-start.1
  35.3 21.3 %collective-permute-start.10 = (f32[16,8,128]{2,1,0:T(8,128)S(1)}, f32[16,8,128]{2,1,0:T(8,128)S(1)}, u32[]{:S(2)}, u32[]{:S(2)}) collective-permute-start(f32[16,8,128]{2,1,0:T(8,128)S(1)} %get-tuple-element.13), channel_id=1, source_target_pairs={{0,8},{8,16},{16,24},{24,0},{1,9},{9,17},{17,25},{25,1},{2,10},{10... | collective-permute-start | bytes 196616 | tf_op jit(solution)/shard_map/ppermute | solution.py:179
  37.3 19.3 %collective-permute-start.11 = (f32[16,8,128]{2,1,0:T(8,128)S(1)}, f32[16,8,128]{2,1,0:T(8,128)S(1)}, u32[]{:S(2)}, u32[]{:S(2)}) collective-permute-start(f32[16,8,128]{2,1,0:T(8,128)S(1)} %get-tuple-element.14), channel_id=1, source_target_pairs={{0,16},{8,24},{16,0},{24,8},{1,17},{9,25},{17,1},{25,9},{2,18},{10... | collective-permute-start | bytes 196616 | tf_op jit(solution)/shard_map/ppermute | solution.py:179
  53.7 4.8 %collective-permute-start.12 = (f32[16,8,128]{2,1,0:T(8,128)S(1)}, f32[16,8,128]{2,1,0:T(8,128)S(1)}, u32[]{:S(2)}, u32[]{:S(2)}) collective-permute-start(f32[16,8,128]{2,1,0:T(8,128)S(1)} %get-tuple-element.15), channel_id=1, source_target_pairs={{0,24},{8,0},{16,8},{24,16},{1,25},{9,1},{17,9},{25,17},{2,26},{10... | collective-permute-start | bytes 196616 | tf_op jit(solution)/shard_map/ppermute | solution.py:179
  56.6 1.9 %copy-start.3 = (f32[16,8,128]{2,1,0:T(8,128)}, f32[16,8,128]{2,1,0:T(8,128)S(1)}, u32[]{:S(2)}) copy-start(f32[16,8,128]{2,1,0:T(8,128)S(1)} %collective-permute-done.10.refs_1_) | copy-start | bytes 196612
  56.6 1.9 %copy-start.4 = (f32[16,8,128]{2,1,0:T(8,128)}, f32[16,8,128]{2,1,0:T(8,128)S(1)}, u32[]{:S(2)}) copy-start(f32[16,8,128]{2,1,0:T(8,128)S(1)} %collective-permute-done.11.refs_2_) | copy-start | bytes 196612
  58.5 0.6 copy-start.5

commit v2 on v1

--- a/solution.py
+++ b/solution.py
@@ -13,22 +13,52 @@
 SLAB = 256
 
 
+def scratch(rows, cols, owned):
+    return [
+        pltpu.VMEM((cols, SLAB, LANES), jnp.float32),
+        pltpu.VMEM((rows, owned, 3, 2 * LANES, LANES), jnp.float32),
+        pltpu.VMEM((rows, 2 * owned, 8, LANES), jnp.float32),
+        pltpu.SMEM((rows * owned,), jnp.int32),
+    ]
+
+
 def pair_kernel(rows, cols, owned, count_ref, pairs_ref, *refs):
-    sources = refs[:cols]
-    targets = refs[cols : cols + rows]
-    outs = refs[cols + rows : cols + 2 * rows]
-    slab, spots, totals = refs[cols + 2 * rows :]
+    sources = refs[:2]
+    targets = refs[2:4]
+    outs = refs[4 : 4 + rows]
+    slab, spots, totals, wanted = refs[4 + rows :]
     my_row = lax.axis_index("row")
     my_col = lax.axis_index("col")
-    spread = sources[0].shape[0]
-    for shift in range(cols):
-        slab[lax.rem(my_col - shift + cols, cols), pl.ds(0, spread), :] = sources[shift][...]
-    for shift in range(rows):
-        spots[lax.rem(my_row - shift + rows, rows)] = 4.0 * targets[shift][...]
-    totals[...] = jnp.zeros_like(totals)
     sides = 8
     stride = 2 * owned
     held = sides * stride
+    spread = 3 * stride
+    for place, mask in enumerate(masks(cols)):
+        stack = sources[place // (cols // 2)]
+        top = (place % (cols // 2)) * (held + spread)
+        origin = lax.bitwise_xor(my_col, mask)
+        slab[origin, pl.ds(0, held), :] = stack[pl.ds(top, held), :]
+        slab[origin, pl.ds(held, spread), :] = 4.0 * stack[pl.ds(top + held, spread), :]
+    for tile in range(rows * owned):
+        wanted[tile] = 0
+    for slot in range(pairs_ref.shape[1]):
+        wanted[pairs_ref[1, slot]] = 1
+    for place, mask in enumerate(masks(rows)):
+        owner = lax.bitwise_xor(my_row, mask)
+        top = (place % (rows // 2)) * spread
+        turned = 4.0 * jnp.transpose(targets[place // (rows // 2)][pl.ds(top, spread), :])
+        for tile in range(owned):
+
+            @pl.when(wanted[tile * rows + owner] == 1)
+            def _():
+                for axis in range(3):
+                    for half in range(2):
+                        lane = axis * stride + 2 * tile + half
+                        spots[owner, tile, axis, pl.ds(LANES * half, LANES), :] = jnp.broadcast_to(
+                            turned[:, lane : lane + 1], (LANES, LANES)
+                        )
+
+    totals[...] = jnp.zeros_like(totals)
 
     def add_pair(slot, carry):
         row_tile = pairs_ref[0, slot]
@@ -36,47 +66,60 @@
         origin = lax.rem(row_tile, cols)
         lane_row = 2 * lax.div(row_tile, cols)
         owner = lax.rem(col_tile, rows)
-        spot_row = 2 * lax.div(col_tile, rows)
-        spot = [
-            [spots[owner, pl.ds(axis * stride + spot_row + half, 1), :] for axis in range(3)]
-            for half in range(2)
-        ]
-        high_parts, low_parts, lhs_parts = [], [], []
+        spot_tile = lax.div(col_tile, rows)
+        lhs_parts = []
+        near = []
         for side in range(2):
             values = slab[origin, pl.ds(lane_row + side, sides, stride=stride), :]
             lead = values.astype(jnp.bfloat16)
             rest = (values - lead.astype(jnp.float32)).astype(jnp.bfloat16)
             lhs_parts.append(jnp.concatenate([lead, rest], axis=0))
-            points = 4.0 * slab[origin, pl.ds(held + lane_row + side, sides, stride=stride), :]
-            turned = jnp.transpose(points)
-            for step in range(LANES // 16):
-                part = turned[16 * step : 16 * step + 16]
-                grid = [jnp.broadcast_to(part[:, axis : axis + 1], (16, LANES)) for axis in range(3)]
-                halves_high, halves_low = [], []
-                for half in range(2):
-                    dx = grid[0] - spot[half][0]
-                    dy = grid[1] - spot[half][1]
-                    dz = grid[2] - spot[half][2]
-                    square = dx * dx + dy * dy + dz * dz
-                    distance = square * lax.rsqrt(jnp.maximum(square, TINY))
-                    left = jnp.maximum(4.0 - distance, 0.0)
-                    left = left * left
-                    weight = left * left * (distance + 1.0)
-                    high = weight.astype(jnp.bfloat16)
-                    halves_high.append(high)
-                    halves_low.append((weight - high.astype(jnp.float32)).astype(jnp.bfloat16))
-                high_parts.append(jnp.concatenate(halves_high, axis=1))
-                low_parts.append(jnp.concatenate(halves_low, axis=1))
+            near.append(
+                [
+                    jnp.broadcast_to(slab[origin, pl.ds(held + axis * stride + lane_row + side, 1), :], (16, LANES))
+                    for axis in range(3)
+                ]
+            )
+        high_parts, low_parts = [], []
+        for step in range(2 * LANES // 16):
+            grid = [spots[owner, spot_tile, axis, pl.ds(16 * step, 16), :] for axis in range(3)]
+            halves_high, halves_low = [], []
+            for side in range(2):
+                dx = grid[0] - near[side][0]
+                dy = grid[1] - near[side][1]
+                dz = grid[2] - near[side][2]
+                square = dx * dx + dy * dy + dz * dz
+                distance = square * lax.rsqrt(jnp.maximum(square, TINY))
+                left = jnp.maximum(4.0 - distance, 0.0)
+                left = left * left
+                weight = left * left * (distance + 1.0)
+                high = weight.astype(jnp.bfloat16)
+                halves_high.append(high)
+                halves_low.append((weight - high.astype(jnp.float32)).astype(jnp.bfloat16))
+            high_parts.append(jnp.concatenate(halves_high, axis=1))
+            low_parts.append(jnp.concatenate(halves_low, axis=1))
         lhs = jnp.concatenate(lhs_parts, axis=1)
-        product = jnp.dot(
-            lhs, jnp.concatenate(high_parts, axis=0), preferred_element_type=jnp.float32
-        ) + jnp.dot(lhs, jnp.concatenate(low_parts, axis=0), preferred_element_type=jnp.float32)
+        dims = (((1,), (1,)), ((), ()))
+        product = lax.dot_general(
+            lhs, jnp.concatenate(high_parts, axis=0), dims, preferred_element_type=jnp.float32
+        ) + lax.dot_general(
+            lhs, jnp.concatenate(low_parts, axis=0), dims, preferred_element_type=jnp.float32
+        )
         summed = product[:sides] + product[sides:]
         for half in range(2):
-            totals[owner, spot_row + half] += summed[:, LANES * half : LANES * half + LANES]
+            totals[owner, 2 * spot_tile + half] += summed[:, LANES * half : LANES * half + LANES]
         return carry
 
-    lax.fori_loop(0, count_ref[0, 0], add_pair, jnp.int32(0))
+    count = count_ref[0, 0]
+    whole = lax.div(count, 8)
+
+    def add_group(step, carry):
+        for part in range(8):
+            add_pair(8 * step + part, carry)
+        return carry
+
+    lax.fori_loop(0, whole, add_group, jnp.int32(0))
+    lax.fori_loop(8 * whole, count, add_pair, jnp.int32(0))
     for shift in range(rows):
         outs[shift][...] = totals[lax.rem(my_row + shift, rows)]
 
@@ -141,6 +184,35 @@
         new_d[place, :] = residual + beta * direction
 
 
+def doubled(blocks, axes, sizes):
+    held = list(blocks)
+    bits = [size // 2 for size in sizes]
+    out = [None] * len(held)
+    while any(bits):
+        live = [at for at, bit in enumerate(bits) if bit]
+        moved = {
+            at: lax.ppermute(held[at], axes[at], [(to, to ^ bits[at]) for to in range(sizes[at])])
+            for at in live
+        }
+        moved = dict(zip(live, lax.optimization_barrier(tuple(moved[at] for at in live))))
+        for at in live:
+            if bits[at] == 1:
+                out[at] = [held[at], moved[at]]
+            else:
+                held[at] = jnp.concatenate([held[at], moved[at]], axis=0)
+            bits[at] //= 2
+    return out
+
+
+def masks(size):
+    found = [0]
+    bit = size // 2
+    while bit:
+        found = found + [mask ^ bit for mask in found]
+        bit //= 2
+    return found
+
+
 def per_device(rows, cols, solution, residual, direction, noise_var, coords, tile_pairs, tile_count):
     sides, owned, _, _, tile_size = direction.shape
     parts = rows * cols
@@ -150,14 +222,7 @@
     flat_d = direction.reshape(-1, LANES)
     flat_c = coords.reshape(-1, LANES)
     mine = jnp.concatenate([flat_d, flat_c], axis=0)
-    sources = [mine] + [
-        lax.ppermute(mine, "col", [(at, (at + shift) % cols) for at in range(cols)])
-        for shift in range(1, cols)
-    ]
-    targets = [flat_c] + [
-        lax.ppermute(flat_c, "row", [(at, (at + shift) % rows) for at in range(rows)])
-        for shift in range(1, rows)
-    ]
+    sources, targets = doubled((mine, flat_c), ("col", "row"), (cols, rows))
     vmem = pl.BlockSpec(memory_space=pltpu.VMEM)
     smem = pl.BlockSpec(memory_space=pltpu.SMEM)
     block = jax.ShapeDtypeStruct((halves, sides, LANES), jnp.float32)
@@ -165,13 +230,9 @@
     partials = pl.pallas_call(
         functools.partial(pair_kernel, rows, cols, owned),
         out_shape=[block] * rows,
-        in_specs=[smem, smem] + [vmem] * (cols + rows),
+        in_specs=[smem, smem] + [vmem] * 4,
         out_specs=[vmem] * rows,
-        scratch_shapes=[
-            pltpu.VMEM((cols, SLAB, LANES), jnp.float32),
-            pltpu.VMEM((rows,) + flat_c.shape, jnp.float32),
-            pltpu.VMEM((rows, halves, sides, LANES), jnp.float32),
-        ],
+        scratch_shapes=scratch(rows, cols, owned),
         compiler_params=pltpu.CompilerParams(vmem_limit_bytes=32 << 20),
         name="pairs",
     )(tile_count, tile_pairs.reshape(2, -1), *sources, *targets)
@@ -185,6 +246,7 @@
         in_specs=[vmem] * (3 + rows),
         out_specs=[vmem] * 2,
         scratch_shapes=[pltpu.VMEM((LANES, LANES), jnp.float32)],
+        compiler_params=pltpu.CompilerParams(vmem_limit_bytes=4 << 20),
         name="sums",
     )(flat_r, flat_d, noise_var.reshape(-1, LANES), *partials)
     stats = lax.all_to_all(stats, ("row", "col"), 0, 0, tiled=True)
@@ -193,6 +255,7 @@
         out_shape=[flat] * 3,
         in_specs=[vmem] * 5,
         out_specs=[vmem] * 3,
+        compiler_params=pltpu.CompilerParams(vmem_limit_bytes=4 << 20),
         name="step",
     )(stats, applied, flat_x, flat_r, flat_d)
     return tuple(new.reshape(direction.shape) for new in (new_x, new_r, new_d))

time: 74.8 us -> 53.2 us (0.71)
  starting transfers between devices: 32.7 us -> 19.2 us
  waiting for transfers between devices: 11.5 us -> 7.56 us
  Pallas kernels: 15 us -> 11.3 us
  local copies, waits for them, and re-layouts: 1.26 us -> 0.03 us
  blocking collectives: 11.8 us -> 12.6 us
    ppermute x3, starting transfers between devices: 21.3 us -> 10.5 us  [per_device(): lax.ppermute(partials[shift], 'row', [(at, (at + shift) % rows) for at in...]
    ppermute x10 -> x5, waiting for transfers between devices: 9.6 us -> 5.66 us  [doubled(): lax.ppermute(held[at], axes[at], [(to, to ^ bits[at]) for to in range(siz...]
    ppermute x10 -> x5, starting transfers between devices: 11.4 us -> 8.76 us  [doubled(): lax.ppermute(held[at], axes[at], [(to, to ^ bits[at]) for to in range(siz...]
    pallas_call x1, Pallas kernels: 1.82 us -> 0.2 us  [per_device(): pl.pallas_call(functools.partial(sums_kernel, rows, parts), out_shape=[bl...]
    pallas_call x1, Pallas kernels: 11.4 us -> 10.2 us  [per_device(): pl.pallas_call(functools.partial(pair_kernel, rows, cols, owned), out_sha...]
    unnamed x12, local copies, waits for them, and re-layouts: 1.26 us -> 0.03 us
    pallas_call x1, Pallas kernels: 1.78 us -> 0.83 us  [per_device(): pl.pallas_call(step_kernel, out_shape=[flat] * 3, in_specs=[vmem] * 5, ou...]
    all_to_all x1, blocking collectives: 11.8 us -> 12.6 us  [per_device(): stats = lax.all_to_all(stats, ('row', 'col'), 0, 0, tiled=True)]
  transfers between devices with their start and end apart: 13 -> 8, of which waited for: 6 -> 4; matrix products, arithmetic and copies ran while one was open for 0% -> 0% of each run, Pallas kernels for 0% -> 0%
where the time goes in v2:
time: 53.2 us; the launch traced here: 53 us
  starting transfers between devices  19.2 us (36%)
  blocking collectives  12.6 us (24%)
  Pallas kernels  11.3 us (21%)
  waiting for transfers between devices  7.56 us (14%)
  between operations  1.35 us (3%)
  other arithmetic  0.95 us (2%)
    all_to_all x1, blocking collectives, per_device(): stats = lax.all_to_all(stats, ('row', 'col'), 0, 0, tiled=True)  12.6 us
    ppermute x3, starting transfers between devices, per_device(): lax.ppermute(partials[shift], 'row', [(at, (at + shift) % rows) for at in...  10.5 us
    pallas_call x1, Pallas kernels, per_device(): pl.pallas_call(functools.partial(pair_kernel, rows, cols, owned), out_sha...  10.2 us
    ppermute x5, starting transfers between devices, doubled(): lax.ppermute(held[at], axes[at], [(to, to ^ bits[at]) for to in range(siz...  8.76 us
    ppermute x5, waiting for transfers between devices, doubled(): lax.ppermute(held[at], axes[at], [(to, to ^ bits[at]) for to in range(siz...  5.66 us
    ppermute x3, waiting for transfers between devices, per_device(): lax.ppermute(partials[shift], 'row', [(at, (at + shift) % rows) for at in...  1.9 us
  transfers between devices with their start and end apart: 8, of which 4 were waited for; matrix products, arithmetic and copies ran while one was open for 0% of the time, Pallas kernels for 0%

profile of v2, /device:TPU:0, one launch (start us, length us, event | category | flops | bytes accessed | tf_op | source)
XLA Modules:
  0.0 53.0 jit_solution(7831798057287538697)
XLA Ops:
  0.6 0.0 copy-start.5
  0.6 0.0 copy-start
  0.7 0.9 %pad_maximum_fusion.2 = f32[176,128]{1,0:T(8,128)S(1)} fusion(f32[48,128]{1,0:T(8,128)} %bitcast.25, f32[128,128]{1,0:T(8,128)} %bitcast.13), kind=kLoop, calls=%fused_computation.2 | loop fusion | flops 22528 | bytes 180224 | tf_op jit(solution)/shard_map/concatenate | solution.py:224
  1.6 3.0 %collective-permute-start = (f32[176,128]{1,0:T(8,128)S(1)}, f32[176,128]{1,0:T(8,128)S(1)}, u32[]{:S(2)}, u32[]{:S(2)}) collective-permute-start(f32[176,128]{1,0:T(8,128)S(1)} %pad_maximum_fusion.2), channel_id=1, source_target_pairs={{0,4},{1,5},{2,6},{3,7},{4,0},{5,1},{6,2},{7,3},{8,12},{9,13},{10,... | collective-permute-start | bytes 270344 | tf_op jit(solution)/shard_map/ppermute | solution.py:194
  4.5 0.0 copy-done.5
  4.5 2.6 %collective-permute-start.1 = (f32[48,128]{1,0:T(8,128)S(1)}, f32[48,128]{1,0:T(8,128)S(1)}, u32[]{:S(2)}, u32[]{:S(2)}) collective-permute-start(f32[48,128]{1,0:T(8,128)S(1)} %bitcast.26), channel_id=1, source_target_pairs={{0,16},{8,24},{16,0},{24,8},{1,17},{9,25},{17,1},{25,9},{2,18},{10... | collective-permute-start | bytes 73736 | tf_op jit(solution)/shard_map/ppermute | solution.py:194
  7.1 2.1 %collective-permute-done.1 = f32[48,128]{1,0:T(8,128)S(1)} collective-permute-done((f32[48,128]{1,0:T(8,128)S(1)}, f32[48,128]{1,0:T(8,128)S(1)}, u32[]{:S(2)}, u32[]{:S(2)}) %collective-permute-start.1) | collective-permute-done | bytes 24608 | tf_op jit(solution)/shard_map/ppermute | solution.py:194
  9.3 0.0 collective-permute-done
  9.3 0.0 copy-done
  9.3 1.6 %collective-permute-start.2 = (f32[352,128]{1,0:T(8,128)S(1)}, f32[352,128]{1,0:T(8,128)S(1)}, u32[]{:S(2)}, u32[]{:S(2)}) collective-permute-start(f32[352,128]{1,0:T(8,128)S(1)} %pad_maximum_fusion.1), channel_id=1, source_target_pairs={{0,2},{1,3},{2,0},{3,1},{4,6},{5,7},{6,4},{7,5},{8,10},{9,11},{10,... | collective-permute-start | bytes 540680 | tf_op jit(solution)/shard_map/ppermute | solution.py:194
  10.8 1.6 %collective-permute-start.3 = (f32[96,128]{1,0:T(8,128)S(1)}, f32[96,128]{1,0:T(8,128)S(1)}, u32[]{:S(2)}, u32[]{:S(2)}) collective-permute-start(f32[96,128]{1,0:T(8,128)S(1)} %pad_maximum_fusion.3.refs_2_), channel_id=1, source_target_pairs={{0,8},{8,0},{16,24},{24,16},{1,9},{9,1},{17,25},{25,17},{2,10},{10... | collective-permute-start | bytes 147464 | tf_op jit(solution)/shard_map/ppermute | solution.py:194
  12.4 2.5 %collective-permute-done.3.refs_3_ = f32[96,128]{1,0:T(8,128)S(1)} collective-permute-done((f32[96,128]{1,0:T(8,128)S(1)}, f32[96,128]{1,0:T(8,128)S(1)}, u32[]{:S(2)}, u32[]{:S(2)}) %collective-permute-start.3) | collective-permute-done | bytes 49184 | tf_op jit(solution)/shard_map/ppermute | solution.py:194
  14.9 0.0 collective-permute-done.2
  15.0 0.1 collective-permute-start.4
  15.7 0.0 copy-start.4
  15.7 1.0 %collective-permute-done.4.refs_1_ = f32[704,128]{1,0:T(8,128)S(1)} collective-permute-done((f32[704,128]{1,0:T(8,128)S(1)}, f32[704,128]{1,0:T(8,128)S(1)}, u32[]{:S(2)}, u32[]{:S(2)}) %collective-permute-start.4) | collective-permute-done | bytes 360480 | tf_op jit(solution)/shard_map/ppermute | solution.py:194
  16.7 0.0 copy-done.4
  16.7 0.0 copy-start.1
  16.7 10.2 %pairs.1 = (f32[16,8,128]{2,1,0:T(8,128)S(1)}, f32[16,8,128]{2,1,0:T(8,128)S(1)}, f32[16,8,128]{2,1,0:T(8,128)S(1)}, f32[16,8,128]{2,1,0:T(8,128)S(1)}) custom-call(s32[1,1]{1,0:T(1,128)S(6)} %copy.17.count_ref, s32[2,64]{1,0:T(2,128)S(1)} %bitcast.24, f32[704,128]{1,0:T(8,128)S(1)} %pad_maximum_fusion.refs_0_, ...), custom_call_target="tpu_custom_call" | custom-call | tf_op jit(solution)/shard_map/pairs/pallas_call | solution.py:230
  26.9 0.0 copy-start.3
  27.0 1.8 %collective-permute-start.5 = (f32[16,8,128]{2,1,0:T(8,128)S(1)}, f32[16,8,128]{2,1,0:T(8,128)S(1)}, u32[]{:S(2)}, u32[]{:S(2)}) collective-permute-start(f32[16,8,128]{2,1,0:T(8,128)S(1)} %get-tuple-element.21), channel_id=1, source_target_pairs={{0,8},{8,16},{16,24},{24,0},{1,9},{9,17},{17,25},{25,1},{2,10},{10... | collective-permute-start | bytes 196616 | tf_op jit(solution)/shard_map/ppermute | solution.py:240
  28.7 5.9 %collective-permute-start.6 = (f32[16,8,128]{2,1,0:T(8,128)S(1)}, f32[16,8,128]{2,1,0:T(8,128)S(1)}, u32[]{:S(2)}, u32[]{:S(2)}) collective-permute-start(f32[16,8,128]{2,1,0:T(8,128)S(1)} %get-tuple-element.22), channel_id=1, source_target_pairs={{0,16},{8,24},{16,0},{24,8},{1,17},{9,25},{17,1},{25,9},{2,18},{10... | collective-permute-start | bytes 196616 | tf_op jit(solution)/shard_map/ppermute | solution.py:240
  34.6 2.8 %collective-permute-start.7 = (f32[16,8,128]{2,1,0:T(8,128)S(1)}, f32[16,8,128]{2,1,0:T(8,128)S(1)}, u32[]{:S(2)}, u32[]{:S(2)}) collective-permute-start(f32[16,8,128]{2,1,0:T(8,128)S(1)} %get-tuple-element.23), channel_id=1, source_target_pairs={{0,24},{8,0},{16,8},{24,16},{1,25},{9,1},{17,9},{25,17},{2,26},{10... | collective-permute-start | bytes 196616 | tf_op jit(solution)/shard_map/ppermute | solution.py:240
  37.4 0.0 collective-permute-done.5.refs_1_
  37.4 0.0 collective-permute-done.6.refs_2_
  37.4 1.9 %collective-permute-done.7.refs_3_ = f32[16,8,128]{2,1,0:T(8,128)S(1)} collective-permute-done((f32[16,8,128]{2,1,0:T(8,128)S(1)}, f32[16,8,128]{2,1,0:T(8,128)S(1)}, u32[]{:S(2)}, u32[]{:S(2)}) %collective-permute-start.7) | collective-permute-done | bytes 65568 | tf_op jit(solution)/shard_map/ppermute | solution.py:240
  39.3 0.0 copy-done.1
  39.4 0.0 copy-done.3
  39.4 0.0 copy-start.2
  39.4 0.2 sums.1
  39.6 12.6 %all_to_all.11 = f32[32,1,128]{2,1,0:T(1,128)S(1)} all-to-all(f32[32,1,128]{2,1,0:T(1,128)S(1)} %bitcast.22), channel_id=1, replica_groups=mesh['row'=4,'col'=8] {'row','col'}, dimensions={0} | all-to-all | bytes 32768 | tf_op jit(solution)/shard_map/all_to_all | solution.py:252
  52.2 0.0 copy-done.2
  52.2 0.8 %step.1 = (f32[128,128]{1,0:T(8,128)}, f32[128,128]{1,0:T(8,128)}, f32[128,128]{1,0:T(8,128)}) custom-call(f32[32,128]{1,0:T(8,128)S(1)} %bitcast.21, f32[16,8,128]{2,1,0:T(8,128)S(1)} %get-tuple-element.25.applied_ref, f32[128,128]{1,0:T(8,128)S(1)} %bitcast.20, f32[128,128]{1,0:T(8,128)S(1)} %bitcast.19, f32[128,128]{1,0:T(8,128)S(1)} %bitcast.17), custom_call_target="tpu_custom_call" | custom-call | tf_op jit(solution)/shard_map/step/pallas_call | solution.py:253
  (3 shorter events, 0.0 us)
Async XLA Ops:
  0.6 3.9 %copy-start.5 = (f32[3,8,1,1,256]{4,3,2,1,0:T(1,128)S(1)}, f32[3,8,1,1,256]{4,3,2,1,0:T(1,128)}, u32[]{:S(2)}) copy-start(f32[3,8,1,1,256]{4,3,2,1,0:T(1,128)} %param.11) | copy-start | bytes 73732
  0.6 8.6 %copy-start = (f32[8,8,1,1,256]{4,3,2,1,0:T(1,128)S(1)}, f32[8,8,1,1,256]{4,3,2,1,0:T(1,128)}, u32[]{:S(2)}) copy-start(f32[8,8,1,1,256]{4,3,2,1,0:T(1,128)} %param.9) | copy-start | bytes 196612
  1.6 7.7 %collective-permute-start = (f32[176,128]{1,0:T(8,128)S(1)}, f32[176,128]{1,0:T(8,128)S(1)}, u32[]{:S(2)}, u32[]{:S(2)}) collective-permute-start(f32[176,128]{1,0:T(8,128)S(1)} %pad_maximum_fusion.2), channel_id=1, source_target_pairs={{0,4},{1,5},{2,6},{3,7},{4,0},{5,1},{6,2},{7,3},{8,12},{9,13},{10,... | collective-permute-start | bytes 270344 | tf_op jit(solution)/shard_map/ppermute | solution.py:194
  4.5 4.7 %collective-permute-start.1 = (f32[48,128]{1,0:T(8,128)S(1)}, f32[48,128]{1,0:T(8,128)S(1)}, u32[]{:S(2)}, u32[]{:S(2)}) collective-permute-start(f32[48,128]{1,0:T(8,128)S(1)} %bitcast.26), channel_id=1, source_target_pairs={{0,16},{8,24},{16,0},{24,8},{1,17},{9,25},{17,1},{25,9},{2,18},{10... | collective-permute-start | bytes 73736 | tf_op jit(solution)/shard_map/ppermute | solution.py:194
  9.3 5.7 %collective-permute-start.2 = (f32[352,128]{1,0:T(8,128)S(1)}, f32[352,128]{1,0:T(8,128)S(1)}, u32[]{:S(2)}, u32[]{:S(2)}) collective-permute-start(f32[352,128]{1,0:T(8,128)S(1)} %pad_maximum_fusion.1), channel_id=1, source_target_pairs={{0,2},{1,3},{2,0},{3,1},{4,6},{5,7},{6,4},{7,5},{8,10},{9,11},{10,... | collective-permute-start | bytes 540680 | tf_op jit(solution)/shard_map/ppermute | solution.py:194
  10.8 4.1 %collective-permute-start.3 = (f32[96,128]{1,0:T(8,128)S(1)}, f32[96,128]{1,0:T(8,128)S(1)}, u32[]{:S(2)}, u32[]{:S(2)}) collective-permute-start(f32[96,128]{1,0:T(8,128)S(1)} %pad_maximum_fusion.3.refs_2_), channel_id=1, source_target_pairs={{0,8},{8,0},{16,24},{24,16},{1,9},{9,1},{17,25},{25,17},{2,10},{10... | collective-permute-start | bytes 147464 | tf_op jit(solution)/shard_map/ppermute | solution.py:194
  15.0 1.7 %collective-permute-start.4 = (f32[704,128]{1,0:T(8,128)S(1)}, f32[704,128]{1,0:T(8,128)S(1)}, u32[]{:S(2)}, u32[]{:S(2)}) collective-permute-start(f32[704,128]{1,0:T(8,128)S(1)} %pad_maximum_fusion.refs_0_), channel_id=1, source_target_pairs={{0,1},{1,0},{2,3},{3,2},{4,5},{5,4},{6,7},{7,6},{8,9},{9,8},{10,11... | collective-permute-start | bytes 1081352 | tf_op jit(solution)/shard_map/ppermute | solution.py:194
  15.7 1.0 %copy-start.4 = (s32[2,1,1,64]{3,2,1,0:T(1,128)S(1)}, s32[2,1,1,64]{3,2,1,0:T(1,128)}, u32[]{:S(2)}) copy-start(s32[2,1,1,64]{3,2,1,0:T(1,128)} %param.12) | copy-start | bytes 1540
  16.7 22.6 %copy-start.1 = (f32[8,8,1,1,256]{4,3,2,1,0:T(1,128)S(1)}, f32[8,8,1,1,256]{4,3,2,1,0:T(1,128)}, u32[]{:S(2)}) copy-start(f32[8,8,1,1,256]{4,3,2,1,0:T(1,128)} %param.8) | copy-start | bytes 196612
  26.9 12.4 %copy-start.3 = (f32[8,1,1,256]{3,2,1,0:T(1,128)S(1)}, f32[8,1,1,256]{3,2,1,0:T(1,128)}, u32[]{:S(2)}) copy-start(f32[8,1,1,256]{3,2,1,0:T(1,128)} %param.10) | copy-start | bytes 24580
  27.0 10.5 %collective-permute-start.5 = (f32[16,8,128]{2,1,0:T(8,128)S(1)}, f32[16,8,128]{2,1,0:T(8,128)S(1)}, u32[]{:S(2)}, u32[]{:S(2)}) collective-permute-start(f32[16,8,128]{2,1,0:T(8,128)S(1)} %get-tuple-element.21), channel_id=1, source_target_pairs={{0,8},{8,16},{16,24},{24,0},{1,9},{9,17},{17,25},{25,1},{2,10},{10... | collective-permute-start | bytes 196616 | tf_op jit(solution)/shard_map/ppermute | solution.py:240
  28.7 8.7 %collective-permute-start.6 = (f32[16,8,128]{2,1,0:T(8,128)S(1)}, f32[16,8,128]{2,1,0:T(8,128)S(1)}, u32[]{:S(2)}, u32[]{:S(2)}) collective-permute-start(f32[16,8,128]{2,1,0:T(8,128)S(1)} %get-tuple-element.22), channel_id=1, source_target_pairs={{0,16},{8,24},{16,0},{24,8},{1,17},{9,25},{17,1},{25,9},{2,18},{10... | collective-permute-start | bytes 196616 | tf_op jit(solution)/shard_map/ppermute | solution.py:240
  34.6 4.8 %collective-permute-start.7 = (f32[16,8,128]{2,1,0:T(8,128)S(1)}, f32[16,8,128]{2,1,0:T(8,128)S(1)}, u32[]{:S(2)}, u32[]{:S(2)}) collective-permute-start(f32[16,8,128]{2,1,0:T(8,128)S(1)} %get-tuple-element.23), channel_id=1, source_target_pairs={{0,24},{8,0},{16,8},{24,16},{1,25},{9,1},{17,9},{25,17},{2,26},{10... | collective-permute-start | bytes 196616 | tf_op jit(solution)/shard_map/ppermute | solution.py:240
  39.4 12.8 %copy-start.2 = (f32[8,8,1,1,256]{4,3,2,1,0:T(1,128)S(1)}, f32[8,8,1,1,256]{4,3,2,1,0:T(1,128)}, u32[]{:S(2)}) copy-start(f32[8,8,1,1,256]{4,3,2,1,0:T(1,128)} %param.7) | copy-start | bytes 196612
